TPU v7x, 256 devices: a whole 4x4x8 slice. The times are simulated.
256 devices in a mesh: panel: 8 (over z), rows: 32 (over y, x, core).
Axes of the slice: x: 4, y: 4, z: 8, core: 2. Of those that a mesh axis runs over, the one named last changes fastest.
Arguments:
- rhs_diag: bfloat16 [8, 8192, 128], P(None, 'rows'), may hold values from -6 to 6
- rhs_tall: bfloat16 [8, 16384, 128], P('panel', 'rows'), may hold values from -6 to 6
- diag_inverse: bfloat16 [8, 1024, 1024], P('panel'), may hold values from -0.1875 to 0.1875
- coupling: bfloat16 [8, 8192, 1024], P('panel', 'rows'), may hold values from -0.09375 to 0.09375
- tall_blocks: bfloat16 [8, 128, 128, 1024], P('panel', 'rows'), may hold values from -0.125 to 0.125
- sparsity: int32 [128, 8], P('rows', 'panel'), may hold values 0 or 1
Outputs:
- solution: float32 [8, 8, 1024, 128], P('panel', None, 'rows')
- tall_residual: float32 [8, 16384, 128], P('panel', 'rows')
All inputs are finite; a program needn't handle non-finite values. No bound on the sum of `sparsity` on one device may be relied on, other than what follows from the above.
Results may differ from a plain program's by a relative error of at most 0.0085.
Values may be sent and summed in bfloat16 or wider, within the bound.
No kernel may reach another device: no remote copies, remote signals or barrier semaphores. Data moves between devices by JAX's collectives and lax.ppermute only.
A program may use at most 64 MiB of HBM per device.

v0:
```python
import jax
import jax.numpy as jnp
from jax import lax
from jax.sharding import PartitionSpec as P


def shifted(block, axis, distance):
    devices = range(lax.axis_size(axis))
    route = [(i - distance, i) for i in devices if i - distance in devices]
    return lax.ppermute(block, axis, route)


def per_device(rhs_diag, rhs_tall, diag_inverse, coupling, tall_blocks, sparsity):
    panel_index = lax.axis_index("panel")
    rows_index = lax.axis_index("rows")
    panel_count = lax.axis_size("panel")
    rows_count = lax.axis_size("rows")
    batches, rows_here, columns = rhs_diag.shape
    panel_width = diag_inverse.shape[1]
    slice_rows = panel_width // rows_count
    blocks_here = tall_blocks.shape[1]
    block_rows = tall_blocks.shape[2]
    tall_rows = blocks_here * block_rows
    rows_panel = rows_index * rows_here // panel_width
    offset = jnp.clip(
        rows_index * rows_here - panel_index * panel_width, 0, panel_width - rows_here
    )
    inverse_cols = lax.dynamic_slice_in_dim(diag_inverse[0], offset, rows_here, 1)
    owner = rows_panel == panel_index
    is_later = rows_panel > panel_index
    coupling_here = coupling[0]
    tall_matrix = tall_blocks[0].reshape(tall_rows, panel_width)
    block_mask = jnp.repeat(sparsity[:, 0].astype(jnp.float32), block_rows)[:, None]

    def advance(tick_number, state_now):
        incoming, solutions, stored = state_now
        batch_now = tick_number - panel_index
        active = (batch_now >= 0) & (batch_now < batches)
        batch_safe = jnp.clip(batch_now, 0, batches - 1)
        rhs_now = lax.dynamic_index_in_dim(rhs_diag, batch_safe, 0, keepdims=False).astype(
            jnp.float32
        )
        reduced = (rhs_now - incoming).astype(jnp.bfloat16)
        partial_value = jnp.dot(inverse_cols, reduced, preferred_element_type=jnp.float32)
        partial_value = jnp.where(owner, partial_value, jnp.float32(0.0))
        summed_all = lax.psum(partial_value, "rows")
        own_rows = lax.dynamic_slice_in_dim(summed_all, rows_index * slice_rows, slice_rows, 0)
        solved = summed_all.astype(jnp.bfloat16)
        previous = lax.dynamic_index_in_dim(solutions, batch_safe, 0, keepdims=False)
        solutions = lax.dynamic_update_index_in_dim(
            solutions, jnp.where(active, own_rows, previous), batch_safe, 0
        )
        update = jnp.dot(coupling_here, solved, preferred_element_type=jnp.float32)
        outgoing = incoming + jnp.where(is_later, update, jnp.float32(0.0))
        earlier = lax.dynamic_index_in_dim(stored, batch_safe, 0, keepdims=False)
        stored = lax.dynamic_update_index_in_dim(
            stored, jnp.where(active, solved, earlier), batch_safe, 0
        )
        incoming = shifted(outgoing, "panel", 1)
        return (incoming, solutions, stored)

    stored = jnp.zeros((batches, panel_width, columns), jnp.bfloat16)
    initial = (
        jnp.zeros((rows_here, columns), jnp.float32),
        jnp.zeros((batches, slice_rows, columns), jnp.float32),
        stored,
    )
    tick_count = batches + panel_count - 1
    incoming, solutions, stored = lax.fori_loop(0, tick_count, advance, initial)
    tall_terms = (
        jnp.einsum("rw,bws->brs", tall_matrix, stored, preferred_element_type=jnp.float32)
        * block_mask
    )
    summed = lax.psum_scatter(tall_terms, "panel", scatter_dimension=0, tiled=True)
    tall_residual = rhs_tall.astype(jnp.float32) - summed
    return (solutions[None], tall_residual)


def solution(mesh):
    placed = (
        P(None, "rows", None),
        P("panel", "rows", None),
        P("panel", None, None),
        P("panel", "rows", None),
        P("panel", "rows", None, None),
        P("rows", "panel"),
    )
    return jax.shard_map(
        per_device,
        mesh=mesh,
        in_specs=placed,
        out_specs=(P("panel", None, "rows", None), P("panel", "rows", None)),
        check_vma=False,
    )
```

profile of v0, /device:TPU:2, one launch (start us, length us, event | category | flops | bytes accessed | tf_op | source)
XLA Modules:
  0.0 1989.9 jit_solution(4910491097746578890)
XLA Ops:
  12.2 1919.9 %while.19 = (s32[]{:T(128)}, f32[256,128]{0,1:T(8,128)S(1)}, f32[8,32,128]{2,1,0:T(8,128)}, bf16[8,1024,128]{1,2,0:T(8,128)(2,1)}, pred[]{:T(512)}, /*index=5*/p...) while((s32[]{:T(128)}, f32[256,128]{0,1:T(8,128)S(1)}, ...), condition=%wide.region_2.3_spmd, body=%wide.region_0.2_spmd.sunk | while | flops 135041024 | bytes 8307022 | solution.py:69
  16.7 115.6 %all-reduce.2.cloned.1.call-done = f32[1024,128]{0,1:T(8,128)} async-done(((f32[1024,128]{0,1:T(8,128)}), f32[1024,128]{0,1:T(8,128)}) %all-reduce.2.cloned.1.call-update) | async-done | bytes 524304 | tf_op jit(solution)/shard_map/while/body/eval_jaxpr/psum | solution.py:46
  145.8 114.6 %all-reduce.2.cloned.1.call-done = f32[1024,128]{0,1:T(8,128)} async-done(((f32[1024,128]{0,1:T(8,128)}), f32[1024,128]{0,1:T(8,128)}) %all-reduce.2.cloned.1.call-update) | async-done | bytes 524304 | tf_op jit(solution)/shard_map/while/body/eval_jaxpr/psum | solution.py:46
  273.9 114.6 %all-reduce.2.cloned.1.call-done = f32[1024,128]{0,1:T(8,128)} async-done(((f32[1024,128]{0,1:T(8,128)}), f32[1024,128]{0,1:T(8,128)}) %all-reduce.2.cloned.1.call-update) | async-done | bytes 524304 | tf_op jit(solution)/shard_map/while/body/eval_jaxpr/psum | solution.py:46
  401.9 114.3 %all-reduce.2.cloned.1.call-done = f32[1024,128]{0,1:T(8,128)} async-done(((f32[1024,128]{0,1:T(8,128)}), f32[1024,128]{0,1:T(8,128)}) %all-reduce.2.cloned.1.call-update) | async-done | bytes 524304 | tf_op jit(solution)/shard_map/while/body/eval_jaxpr/psum | solution.py:46
  529.7 114.3 %all-reduce.2.cloned.1.call-done = f32[1024,128]{0,1:T(8,128)} async-done(((f32[1024,128]{0,1:T(8,128)}), f32[1024,128]{0,1:T(8,128)}) %all-reduce.2.cloned.1.call-update) | async-done | bytes 524304 | tf_op jit(solution)/shard_map/while/body/eval_jaxpr/psum | solution.py:46
  646.0 3.5 collective-permute-start
  657.5 114.2 %all-reduce.2.cloned.1.call-done = f32[1024,128]{0,1:T(8,128)} async-done(((f32[1024,128]{0,1:T(8,128)}), f32[1024,128]{0,1:T(8,128)}) %all-reduce.2.cloned.1.call-update) | async-done | bytes 524304 | tf_op jit(solution)/shard_map/while/body/eval_jaxpr/psum | solution.py:46
  785.2 114.6 %all-reduce.2.cloned.1.call-done = f32[1024,128]{0,1:T(8,128)} async-done(((f32[1024,128]{0,1:T(8,128)}), f32[1024,128]{0,1:T(8,128)}) %all-reduce.2.cloned.1.call-update) | async-done | bytes 524304 | tf_op jit(solution)/shard_map/while/body/eval_jaxpr/psum | solution.py:46
  901.8 3.5 collective-permute-start
  913.2 114.6 %all-reduce.2.cloned.1.call-done = f32[1024,128]{0,1:T(8,128)} async-done(((f32[1024,128]{0,1:T(8,128)}), f32[1024,128]{0,1:T(8,128)}) %all-reduce.2.cloned.1.call-update) | async-done | bytes 524304 | tf_op jit(solution)/shard_map/while/body/eval_jaxpr/psum | solution.py:46
  1041.3 114.6 %all-reduce.2.cloned.1.call-done = f32[1024,128]{0,1:T(8,128)} async-done(((f32[1024,128]{0,1:T(8,128)}), f32[1024,128]{0,1:T(8,128)}) %all-reduce.2.cloned.1.call-update) | async-done | bytes 524304 | tf_op jit(solution)/shard_map/while/body/eval_jaxpr/psum | solution.py:46
  1169.4 114.3 %all-reduce.2.cloned.1.call-done = f32[1024,128]{0,1:T(8,128)} async-done(((f32[1024,128]{0,1:T(8,128)}), f32[1024,128]{0,1:T(8,128)}) %all-reduce.2.cloned.1.call-update) | async-done | bytes 524304 | tf_op jit(solution)/shard_map/while/body/eval_jaxpr/psum | solution.py:46
  1285.7 3.5 collective-permute-start
  1297.1 114.6 %all-reduce.2.cloned.1.call-done = f32[1024,128]{0,1:T(8,128)} async-done(((f32[1024,128]{0,1:T(8,128)}), f32[1024,128]{0,1:T(8,128)}) %all-reduce.2.cloned.1.call-update) | async-done | bytes 524304 | tf_op jit(solution)/shard_map/while/body/eval_jaxpr/psum | solution.py:46
  1413.8 3.5 collective-permute-start
  1425.2 114.3 %all-reduce.2.cloned.1.call-done = f32[1024,128]{0,1:T(8,128)} async-done(((f32[1024,128]{0,1:T(8,128)}), f32[1024,128]{0,1:T(8,128)}) %all-reduce.2.cloned.1.call-update) | async-done | bytes 524304 | tf_op jit(solution)/shard_map/while/body/eval_jaxpr/psum | solution.py:46
  1541.6 3.5 collective-permute-start
  1553.0 114.6 %all-reduce.2.cloned.1.call-done = f32[1024,128]{0,1:T(8,128)} async-done(((f32[1024,128]{0,1:T(8,128)}), f32[1024,128]{0,1:T(8,128)}) %all-reduce.2.cloned.1.call-update) | async-done | bytes 524304 | tf_op jit(solution)/shard_map/while/body/eval_jaxpr/psum | solution.py:46
  1669.6 3.5 collective-permute-start
  1681.0 114.2 %all-reduce.2.cloned.1.call-done = f32[1024,128]{0,1:T(8,128)} async-done(((f32[1024,128]{0,1:T(8,128)}), f32[1024,128]{0,1:T(8,128)}) %all-reduce.2.cloned.1.call-update) | async-done | bytes 524304 | tf_op jit(solution)/shard_map/while/body/eval_jaxpr/psum | solution.py:46
  1808.8 114.3 %all-reduce.2.cloned.1.call-done = f32[1024,128]{0,1:T(8,128)} async-done(((f32[1024,128]{0,1:T(8,128)}), f32[1024,128]{0,1:T(8,128)}) %all-reduce.2.cloned.1.call-update) | async-done | bytes 524304 | tf_op jit(solution)/shard_map/while/body/eval_jaxpr/psum | solution.py:46
  1932.0 4.5 multiply_bitcast_fusion
  1937.5 43.4 %reduce-scatter.2.cloned.1.call-done = f32[1,512,128]{1,2,0:T(8,128)} async-done(((f32[8,512,128]{1,2,0:T(8,128)}), f32[1,512,128]{1,2,0:T(8,128)}) %reduce-scatter.2.cloned.1.call-update) | async-done | bytes 262160 | tf_op jit(solution)/shard_map/reduce_scatter | solution.py:74
  (266 shorter events, 187.8 us)
Async XLA Ops:
  12.2 120.1 %all-reduce.2.cloned.1.call-start = ((), (), s32[]{:S(2)}) async-start(), calls=%async_computation.2 | async-start | bytes 1048576 | tf_op jit(solution)/shard_map/while/body/eval_jaxpr/psum | solution.py:46
  141.2 119.2 %all-reduce.2.cloned.1.call-start = ((), (), s32[]{:S(2)}) async-start(), calls=%async_computation.2 | async-start | bytes 1048576 | tf_op jit(solution)/shard_map/while/body/eval_jaxpr/psum | solution.py:46
  269.3 119.1 %all-reduce.2.cloned.1.call-start = ((), (), s32[]{:S(2)}) async-start(), calls=%async_computation.2 | async-start | bytes 1048576 | tf_op jit(solution)/shard_map/while/body/eval_jaxpr/psum | solution.py:46
  397.4 118.8 %all-reduce.2.cloned.1.call-start = ((), (), s32[]{:S(2)}) async-start(), calls=%async_computation.2 | async-start | bytes 1048576 | tf_op jit(solution)/shard_map/while/body/eval_jaxpr/psum | solution.py:46
  525.1 118.8 %all-reduce.2.cloned.1.call-start = ((), (), s32[]{:S(2)}) async-start(), calls=%async_computation.2 | async-start | bytes 1048576 | tf_op jit(solution)/shard_map/while/body/eval_jaxpr/psum | solution.py:46
  646.0 6.9 collective-permute-start
  652.9 118.8 %all-reduce.2.cloned.1.call-start = ((), (), s32[]{:S(2)}) async-start(), calls=%async_computation.2 | async-start | bytes 1048576 | tf_op jit(solution)/shard_map/while/body/eval_jaxpr/psum | solution.py:46
  780.6 119.1 %all-reduce.2.cloned.1.call-start = ((), (), s32[]{:S(2)}) async-start(), calls=%async_computation.2 | async-start | bytes 1048576 | tf_op jit(solution)/shard_map/while/body/eval_jaxpr/psum | solution.py:46
  908.7 119.1 %all-reduce.2.cloned.1.call-start = ((), (), s32[]{:S(2)}) async-start(), calls=%async_computation.2 | async-start | bytes 1048576 | tf_op jit(solution)/shard_map/while/body/eval_jaxpr/psum | solution.py:46
  1029.8 6.9 collective-permute-start
  1036.7 119.1 %all-reduce.2.cloned.1.call-start = ((), (), s32[]{:S(2)}) async-start(), calls=%async_computation.2 | async-start | bytes 1048576 | tf_op jit(solution)/shard_map/while/body/eval_jaxpr/psum | solution.py:46
  1157.9 6.9 collective-permute-start
  1164.8 118.8 %all-reduce.2.cloned.1.call-start = ((), (), s32[]{:S(2)}) async-start(), calls=%async_computation.2 | async-start | bytes 1048576 | tf_op jit(solution)/shard_map/while/body/eval_jaxpr/psum | solution.py:46
  1285.7 6.9 collective-permute-start
  1292.6 119.1 %all-reduce.2.cloned.1.call-start = ((), (), s32[]{:S(2)}) async-start(), calls=%async_computation.2 | async-start | bytes 1048576 | tf_op jit(solution)/shard_map/while/body/eval_jaxpr/psum | solution.py:46
  1413.8 6.9 collective-permute-start
  1420.7 118.8 %all-reduce.2.cloned.1.call-start = ((), (), s32[]{:S(2)}) async-start(), calls=%async_computation.2 | async-start | bytes 1048576 | tf_op jit(solution)/shard_map/while/body/eval_jaxpr/psum | solution.py:46
  1541.6 6.9 collective-permute-start
  1548.5 119.1 %all-reduce.2.cloned.1.call-start = ((), (), s32[]{:S(2)}) async-start(), calls=%async_computation.2 | async-start | bytes 1048576 | tf_op jit(solution)/shard_map/while/body/eval_jaxpr/psum | solution.py:46
  1669.6 6.9 collective-permute-start
  1676.5 118.8 %all-reduce.2.cloned.1.call-start = ((), (), s32[]{:S(2)}) async-start(), calls=%async_computation.2 | async-start | bytes 1048576 | tf_op jit(solution)/shard_map/while/body/eval_jaxpr/psum | solution.py:46
  1804.2 118.8 %all-reduce.2.cloned.1.call-start = ((), (), s32[]{:S(2)}) async-start(), calls=%async_computation.2 | async-start | bytes 1048576 | tf_op jit(solution)/shard_map/while/body/eval_jaxpr/psum | solution.py:46
  1925.1 6.9 collective-permute-start
  1932.0 48.9 %reduce-scatter.2.cloned.1.call-start = ((), (), s32[]{:S(2)}) async-start(), calls=%async_computation.1 | async-start | bytes 2359296 | tf_op jit(solution)/shard_map/reduce_scatter | solution.py:74
  (25 other events, 164.8 us)
Sparse Core Ops, SparseCore 0:
  16.2 116.0 all-reduce.1
  145.2 115.0 all-reduce.1
  273.3 115.0 all-reduce.1
  401.1 115.0 all-reduce.1
  528.8 115.0 all-reduce.1
  656.6 115.0 all-reduce.1
  784.6 115.0 all-reduce.1
  912.7 115.0 all-reduce.1
  1040.8 115.0 all-reduce.1
  1168.5 115.0 all-reduce.1
  1296.6 115.0 all-reduce.1
  1424.4 115.0 all-reduce.1
  1552.5 115.0 all-reduce.1
  1680.2 115.0 all-reduce.1
  1807.9 115.0 all-reduce.1
Sparse Core Ops, SparseCore 1:
  1936.6 44.3 reduce-scatter.1
where the time goes:
time: 1990 us
  waiting for transfers between devices  1760 us (88%)
  local copies, waits for them, and re-layouts  66.1 us (3%)
  matrix products  51.9 us (3%)
  starting transfers between devices  51.8 us (3%)
  other arithmetic  42.9 us (2%)
    psum x15, waiting for transfers between devices, advance(): summed_all = lax.psum(partial_value, 'rows')  1720 us
    ppermute x15, starting transfers between devices, shifted(): return lax.ppermute(block, axis, route)  51.8 us
    reduce_scatter x1, waiting for transfers between devices, per_device(): lax.psum_scatter(tall_terms, 'panel', scatter_dimension=0, tiled=True)  43.4 us
  transfers between devices with their start and end apart: 31, of which 16 were waited for; matrix products, arithmetic and copies ran while one was open for 4% of the time, Pallas kernels for 0%

commit v1 on v0

--- a/solution.py
+++ b/solution.py
@@ -43,7 +43,11 @@
         reduced = (rhs_now - incoming).astype(jnp.bfloat16)
         partial_value = jnp.dot(inverse_cols, reduced, preferred_element_type=jnp.float32)
         partial_value = jnp.where(owner, partial_value, jnp.float32(0.0))
-        summed_all = lax.psum(partial_value, "rows")
+        summed_all = partial_value
+        for hop in (1, 2, 4, 8, 16):
+            summed_all = summed_all + lax.ppermute(
+                summed_all, "rows", [(dev, dev ^ hop) for dev in range(32)]
+            )
         own_rows = lax.dynamic_slice_in_dim(summed_all, rows_index * slice_rows, slice_rows, 0)
         solved = summed_all.astype(jnp.bfloat16)
         previous = lax.dynamic_index_in_dim(solutions, batch_safe, 0, keepdims=False)

time: 1990 us -> 1090 us (0.55)
  waiting for transfers between devices: 1760 us -> 813 us
  starting transfers between devices: 51.8 us -> 174 us
  matrix products: 51.9 us -> 13.7 us
  local copies, waits for them, and re-layouts: 66.1 us -> 36.6 us
    psum x15 -> x0, waiting for transfers between devices: 1720 us -> none  [advance(): summed_all = lax.psum(partial_value, 'rows')]
    ppermute x0 -> x75, waiting for transfers between devices: none -> 728 us  [advance(): lax.ppermute(summed_all, 'rows', [(dev, dev ^ hop) for dev in range(32)])]
    ppermute x0 -> x75, starting transfers between devices: none -> 96.9 us  [advance(): lax.ppermute(summed_all, 'rows', [(dev, dev ^ hop) for dev in range(32)])]
    ppermute x15, waiting for transfers between devices: 0.04 us -> 35 us  [shifted(): return lax.ppermute(block, axis, route)]
    dot_general x15, matrix products: 30.6 us -> 4.65 us  [advance(): update = jnp.dot(coupling_here, solved, preferred_element_type=jnp.float32)]
    ppermute x15, starting transfers between devices: 51.8 us -> 77 us  [shifted(): return lax.ppermute(block, axis, route)]
    dynamic_slice x30, local copies, waits for them, and re-layouts: 21.8 us -> 1.52 us  [advance(): lax.dynamic_index_in_dim(solutions, batch_safe, 0, keepdims=False)]
  transfers between devices with their start and end apart: 31 -> 91, of which waited for: 16 -> 91; matrix products, arithmetic and copies ran while one was open for 4% -> 2% of each run, Pallas kernels for 0% -> 0%
where the time goes in v1:
time: 1090 us
  waiting for transfers between devices  813 us (75%)
  starting transfers between devices  174 us (16%)
  local copies, waits for them, and re-layouts  36.6 us (3%)
  other arithmetic  34.4 us (3%)
  between operations  14.1 us (1%)
  matrix products  13.7 us (1%)
    ppermute x75, waiting for transfers between devices, advance(): lax.ppermute(summed_all, 'rows', [(dev, dev ^ hop) for dev in range(32)])  728 us
    ppermute x75, starting transfers between devices, advance(): lax.ppermute(summed_all, 'rows', [(dev, dev ^ hop) for dev in range(32)])  96.9 us
    ppermute x15, starting transfers between devices, shifted(): return lax.ppermute(block, axis, route)  77 us
    reduce_scatter x1, waiting for transfers between devices, per_device(): lax.psum_scatter(tall_terms, 'panel', scatter_dimension=0, tiled=True)  49.3 us
    ppermute x15, waiting for transfers between devices, shifted(): return lax.ppermute(block, axis, route)  35 us
    dynamic_update_slice x15, other arithmetic, advance(): lax.dynamic_update_index_in_dim(stored, jnp.where(active, solved, earlier...  27.8 us
  transfers between devices with their start and end apart: 91, of which 91 were waited for; matrix products, arithmetic and copies ran while one was open for 2% of the time, Pallas kernels for 0%

profile of v1, /device:TPU:2, one launch (start us, length us, event | category | flops | bytes accessed | tf_op | source)
XLA Modules:
  0.0 1086.9 jit_solution(10306877320786490651)
XLA Ops:
  10.6 1012.8 %while.19 = (s32[]{:T(128)}, f32[256,128]{0,1:T(8,128)S(1)}, f32[8,32,128]{2,1,0:T(8,128)S(1)}, bf16[8,1024,128]{1,2,0:T(8,128)(2,1)}, pred[]{:T(512)}, /*index=...) while((s32[]{:T(128)}, f32[256,128]{0,1:T(8,128)S(1)}, ...), condition=%wide.region_1.2_spmd, body=%wide.region_0.1_spmd.sunk | while | flops 135565312 | bytes 25018860 | solution.py:73
  30.3 13.4 %collective-permute-done.2 = f32[1024,128]{0,1:T(8,128)S(1)} collective-permute-done((f32[1024,128]{0,1:T(8,128)S(1)}, f32[1024,128]{0,1:T(8,128)S(1)}, u32[]{:S(2)}, u32[]{:S(2)}) %collective-permute-start.2) | collective-permute-done | bytes 524320 | tf_op jit(solution)/shard_map/while/body/eval_jaxpr/ppermute | solution.py:48
  81.4 13.4 %collective-permute-done.1 = f32[1024,128]{0,1:T(8,128)S(1)} collective-permute-done((f32[1024,128]{0,1:T(8,128)S(1)}, f32[1024,128]{0,1:T(8,128)S(1)}, u32[]{:S(2)}, u32[]{:S(2)}) %collective-permute-start.1) | collective-permute-done | bytes 524320 | tf_op jit(solution)/shard_map/while/body/eval_jaxpr/ppermute | solution.py:48
  97.2 12.5 %collective-permute-done.2 = f32[1024,128]{0,1:T(8,128)S(1)} collective-permute-done((f32[1024,128]{0,1:T(8,128)S(1)}, f32[1024,128]{0,1:T(8,128)S(1)}, u32[]{:S(2)}, u32[]{:S(2)}) %collective-permute-start.2) | collective-permute-done | bytes 524320 | tf_op jit(solution)/shard_map/while/body/eval_jaxpr/ppermute | solution.py:48
  148.1 13.4 %collective-permute-done.1 = f32[1024,128]{0,1:T(8,128)S(1)} collective-permute-done((f32[1024,128]{0,1:T(8,128)S(1)}, f32[1024,128]{0,1:T(8,128)S(1)}, u32[]{:S(2)}, u32[]{:S(2)}) %collective-permute-start.1) | collective-permute-done | bytes 524320 | tf_op jit(solution)/shard_map/while/body/eval_jaxpr/ppermute | solution.py:48
  163.8 12.5 %collective-permute-done.2 = f32[1024,128]{0,1:T(8,128)S(1)} collective-permute-done((f32[1024,128]{0,1:T(8,128)S(1)}, f32[1024,128]{0,1:T(8,128)S(1)}, u32[]{:S(2)}, u32[]{:S(2)}) %collective-permute-start.2) | collective-permute-done | bytes 524320 | tf_op jit(solution)/shard_map/while/body/eval_jaxpr/ppermute | solution.py:48
  214.7 13.4 %collective-permute-done.1 = f32[1024,128]{0,1:T(8,128)S(1)} collective-permute-done((f32[1024,128]{0,1:T(8,128)S(1)}, f32[1024,128]{0,1:T(8,128)S(1)}, u32[]{:S(2)}, u32[]{:S(2)}) %collective-permute-start.1) | collective-permute-done | bytes 524320 | tf_op jit(solution)/shard_map/while/body/eval_jaxpr/ppermute | solution.py:48
  230.4 12.5 %collective-permute-done.2 = f32[1024,128]{0,1:T(8,128)S(1)} collective-permute-done((f32[1024,128]{0,1:T(8,128)S(1)}, f32[1024,128]{0,1:T(8,128)S(1)}, u32[]{:S(2)}, u32[]{:S(2)}) %collective-permute-start.2) | collective-permute-done | bytes 524320 | tf_op jit(solution)/shard_map/while/body/eval_jaxpr/ppermute | solution.py:48
  281.4 13.4 %collective-permute-done.1 = f32[1024,128]{0,1:T(8,128)S(1)} collective-permute-done((f32[1024,128]{0,1:T(8,128)S(1)}, f32[1024,128]{0,1:T(8,128)S(1)}, u32[]{:S(2)}, u32[]{:S(2)}) %collective-permute-start.1) | collective-permute-done | bytes 524320 | tf_op jit(solution)/shard_map/while/body/eval_jaxpr/ppermute | solution.py:48
  297.1 12.5 %collective-permute-done.2 = f32[1024,128]{0,1:T(8,128)S(1)} collective-permute-done((f32[1024,128]{0,1:T(8,128)S(1)}, f32[1024,128]{0,1:T(8,128)S(1)}, u32[]{:S(2)}, u32[]{:S(2)}) %collective-permute-start.2) | collective-permute-done | bytes 524320 | tf_op jit(solution)/shard_map/while/body/eval_jaxpr/ppermute | solution.py:48
  348.9 13.4 %collective-permute-done.1 = f32[1024,128]{0,1:T(8,128)S(1)} collective-permute-done((f32[1024,128]{0,1:T(8,128)S(1)}, f32[1024,128]{0,1:T(8,128)S(1)}, u32[]{:S(2)}, u32[]{:S(2)}) %collective-permute-start.1) | collective-permute-done | bytes 524320 | tf_op jit(solution)/shard_map/while/body/eval_jaxpr/ppermute | solution.py:48
  364.6 12.5 %collective-permute-done.2 = f32[1024,128]{0,1:T(8,128)S(1)} collective-permute-done((f32[1024,128]{0,1:T(8,128)S(1)}, f32[1024,128]{0,1:T(8,128)S(1)}, u32[]{:S(2)}, u32[]{:S(2)}) %collective-permute-start.2) | collective-permute-done | bytes 524320 | tf_op jit(solution)/shard_map/while/body/eval_jaxpr/ppermute | solution.py:48
  416.7 13.4 %collective-permute-done.1 = f32[1024,128]{0,1:T(8,128)S(1)} collective-permute-done((f32[1024,128]{0,1:T(8,128)S(1)}, f32[1024,128]{0,1:T(8,128)S(1)}, u32[]{:S(2)}, u32[]{:S(2)}) %collective-permute-start.1) | collective-permute-done | bytes 524320 | tf_op jit(solution)/shard_map/while/body/eval_jaxpr/ppermute | solution.py:48
  484.6 13.4 %collective-permute-done.1 = f32[1024,128]{0,1:T(8,128)S(1)} collective-permute-done((f32[1024,128]{0,1:T(8,128)S(1)}, f32[1024,128]{0,1:T(8,128)S(1)}, u32[]{:S(2)}, u32[]{:S(2)}) %collective-permute-start.1) | collective-permute-done | bytes 524320 | tf_op jit(solution)/shard_map/while/body/eval_jaxpr/ppermute | solution.py:48
  500.3 12.5 %collective-permute-done.2 = f32[1024,128]{0,1:T(8,128)S(1)} collective-permute-done((f32[1024,128]{0,1:T(8,128)S(1)}, f32[1024,128]{0,1:T(8,128)S(1)}, u32[]{:S(2)}, u32[]{:S(2)}) %collective-permute-start.2) | collective-permute-done | bytes 524320 | tf_op jit(solution)/shard_map/while/body/eval_jaxpr/ppermute | solution.py:48
  552.4 13.4 %collective-permute-done.1 = f32[1024,128]{0,1:T(8,128)S(1)} collective-permute-done((f32[1024,128]{0,1:T(8,128)S(1)}, f32[1024,128]{0,1:T(8,128)S(1)}, u32[]{:S(2)}, u32[]{:S(2)}) %collective-permute-start.1) | collective-permute-done | bytes 524320 | tf_op jit(solution)/shard_map/while/body/eval_jaxpr/ppermute | solution.py:48
  568.1 12.5 %collective-permute-done.2 = f32[1024,128]{0,1:T(8,128)S(1)} collective-permute-done((f32[1024,128]{0,1:T(8,128)S(1)}, f32[1024,128]{0,1:T(8,128)S(1)}, u32[]{:S(2)}, u32[]{:S(2)}) %collective-permute-start.2) | collective-permute-done | bytes 524320 | tf_op jit(solution)/shard_map/while/body/eval_jaxpr/ppermute | solution.py:48
  620.3 13.4 %collective-permute-done.1 = f32[1024,128]{0,1:T(8,128)S(1)} collective-permute-done((f32[1024,128]{0,1:T(8,128)S(1)}, f32[1024,128]{0,1:T(8,128)S(1)}, u32[]{:S(2)}, u32[]{:S(2)}) %collective-permute-start.1) | collective-permute-done | bytes 524320 | tf_op jit(solution)/shard_map/while/body/eval_jaxpr/ppermute | solution.py:48
  688.1 13.4 %collective-permute-done.1 = f32[1024,128]{0,1:T(8,128)S(1)} collective-permute-done((f32[1024,128]{0,1:T(8,128)S(1)}, f32[1024,128]{0,1:T(8,128)S(1)}, u32[]{:S(2)}, u32[]{:S(2)}) %collective-permute-start.1) | collective-permute-done | bytes 524320 | tf_op jit(solution)/shard_map/while/body/eval_jaxpr/ppermute | solution.py:48
  756.0 13.4 %collective-permute-done.1 = f32[1024,128]{0,1:T(8,128)S(1)} collective-permute-done((f32[1024,128]{0,1:T(8,128)S(1)}, f32[1024,128]{0,1:T(8,128)S(1)}, u32[]{:S(2)}, u32[]{:S(2)}) %collective-permute-start.1) | collective-permute-done | bytes 524320 | tf_op jit(solution)/shard_map/while/body/eval_jaxpr/ppermute | solution.py:48
  823.8 13.4 %collective-permute-done.1 = f32[1024,128]{0,1:T(8,128)S(1)} collective-permute-done((f32[1024,128]{0,1:T(8,128)S(1)}, f32[1024,128]{0,1:T(8,128)S(1)}, u32[]{:S(2)}, u32[]{:S(2)}) %collective-permute-start.1) | collective-permute-done | bytes 524320 | tf_op jit(solution)/shard_map/while/body/eval_jaxpr/ppermute | solution.py:48
  891.7 13.4 %collective-permute-done.1 = f32[1024,128]{0,1:T(8,128)S(1)} collective-permute-done((f32[1024,128]{0,1:T(8,128)S(1)}, f32[1024,128]{0,1:T(8,128)S(1)}, u32[]{:S(2)}, u32[]{:S(2)}) %collective-permute-start.1) | collective-permute-done | bytes 524320 | tf_op jit(solution)/shard_map/while/body/eval_jaxpr/ppermute | solution.py:48
  959.6 13.4 %collective-permute-done.1 = f32[1024,128]{0,1:T(8,128)S(1)} collective-permute-done((f32[1024,128]{0,1:T(8,128)S(1)}, f32[1024,128]{0,1:T(8,128)S(1)}, u32[]{:S(2)}, u32[]{:S(2)}) %collective-permute-start.1) | collective-permute-done | bytes 524320 | tf_op jit(solution)/shard_map/while/body/eval_jaxpr/ppermute | solution.py:48
  1029.0 49.3 %reduce-scatter.2.cloned.1.call-done = f32[1,512,128]{1,2,0:T(8,128)} async-done(((f32[8,512,128]{1,2,0:T(8,128)}), f32[1,512,128]{1,2,0:T(8,128)}) %reduce-scatter.2.cloned.1.call-update) | async-done | bytes 262160 | tf_op jit(solution)/shard_map/reduce_scatter | solution.py:78
  (431 shorter events, 733.2 us)
Async XLA Ops:
  7.2 1071.1 %reduce-scatter.2.cloned.1.call-start = ((), (), s32[]{:S(2)}) async-start(), calls=%async_computation.1 | async-start | bytes 2359296 | tf_op jit(solution)/shard_map/reduce_scatter | solution.py:78
  14.0 14.6 %collective-permute-start.1 = (f32[1024,128]{0,1:T(8,128)S(1)}, f32[1024,128]{0,1:T(8,128)S(1)}, u32[]{:S(2)}, u32[]{:S(2)}) collective-permute-start(f32[1024,128]{0,1:T(8,128)S(1)} %add.111), channel_id=1, source_target_pairs={{0,2},{1,3},{2,0},{3,1},{4,6},{5,7},{6,4},{7,5},{8,10},{9,11},{10,... | collective-permute-start | bytes 1572872 | tf_op jit(solution)/shard_map/while/body/eval_jaxpr/ppermute | solution.py:48
  28.6 15.0 %collective-permute-start.2 = (f32[1024,128]{0,1:T(8,128)S(1)}, f32[1024,128]{0,1:T(8,128)S(1)}, u32[]{:S(2)}, u32[]{:S(2)}) collective-permute-start(f32[1024,128]{0,1:T(8,128)S(1)} %add.112), channel_id=1, source_target_pairs={{0,4},{1,5},{2,6},{3,7},{4,0},{5,1},{6,2},{7,3},{8,12},{9,13},{10,... | collective-permute-start | bytes 1572872 | tf_op jit(solution)/shard_map/while/body/eval_jaxpr/ppermute | solution.py:48
  80.8 14.1 %collective-permute-start.1 = (f32[1024,128]{0,1:T(8,128)S(1)}, f32[1024,128]{0,1:T(8,128)S(1)}, u32[]{:S(2)}, u32[]{:S(2)}) collective-permute-start(f32[1024,128]{0,1:T(8,128)S(1)} %add.111), channel_id=1, source_target_pairs={{0,2},{1,3},{2,0},{3,1},{4,6},{5,7},{6,4},{7,5},{8,10},{9,11},{10,... | collective-permute-start | bytes 1572872 | tf_op jit(solution)/shard_map/while/body/eval_jaxpr/ppermute | solution.py:48
  94.9 14.7 %collective-permute-start.2 = (f32[1024,128]{0,1:T(8,128)S(1)}, f32[1024,128]{0,1:T(8,128)S(1)}, u32[]{:S(2)}, u32[]{:S(2)}) collective-permute-start(f32[1024,128]{0,1:T(8,128)S(1)} %add.112), channel_id=1, source_target_pairs={{0,4},{1,5},{2,6},{3,7},{4,0},{5,1},{6,2},{7,3},{8,12},{9,13},{10,... | collective-permute-start | bytes 1572872 | tf_op jit(solution)/shard_map/while/body/eval_jaxpr/ppermute | solution.py:48
  147.4 14.1 %collective-permute-start.1 = (f32[1024,128]{0,1:T(8,128)S(1)}, f32[1024,128]{0,1:T(8,128)S(1)}, u32[]{:S(2)}, u32[]{:S(2)}) collective-permute-start(f32[1024,128]{0,1:T(8,128)S(1)} %add.111), channel_id=1, source_target_pairs={{0,2},{1,3},{2,0},{3,1},{4,6},{5,7},{6,4},{7,5},{8,10},{9,11},{10,... | collective-permute-start | bytes 1572872 | tf_op jit(solution)/shard_map/while/body/eval_jaxpr/ppermute | solution.py:48
  161.6 14.7 %collective-permute-start.2 = (f32[1024,128]{0,1:T(8,128)S(1)}, f32[1024,128]{0,1:T(8,128)S(1)}, u32[]{:S(2)}, u32[]{:S(2)}) collective-permute-start(f32[1024,128]{0,1:T(8,128)S(1)} %add.112), channel_id=1, source_target_pairs={{0,4},{1,5},{2,6},{3,7},{4,0},{5,1},{6,2},{7,3},{8,12},{9,13},{10,... | collective-permute-start | bytes 1572872 | tf_op jit(solution)/shard_map/while/body/eval_jaxpr/ppermute | solution.py:48
  214.1 14.1 %collective-permute-start.1 = (f32[1024,128]{0,1:T(8,128)S(1)}, f32[1024,128]{0,1:T(8,128)S(1)}, u32[]{:S(2)}, u32[]{:S(2)}) collective-permute-start(f32[1024,128]{0,1:T(8,128)S(1)} %add.111), channel_id=1, source_target_pairs={{0,2},{1,3},{2,0},{3,1},{4,6},{5,7},{6,4},{7,5},{8,10},{9,11},{10,... | collective-permute-start | bytes 1572872 | tf_op jit(solution)/shard_map/while/body/eval_jaxpr/ppermute | solution.py:48
  228.2 14.7 %collective-permute-start.2 = (f32[1024,128]{0,1:T(8,128)S(1)}, f32[1024,128]{0,1:T(8,128)S(1)}, u32[]{:S(2)}, u32[]{:S(2)}) collective-permute-start(f32[1024,128]{0,1:T(8,128)S(1)} %add.112), channel_id=1, source_target_pairs={{0,4},{1,5},{2,6},{3,7},{4,0},{5,1},{6,2},{7,3},{8,12},{9,13},{10,... | collective-permute-start | bytes 1572872 | tf_op jit(solution)/shard_map/while/body/eval_jaxpr/ppermute | solution.py:48
  280.8 14.1 %collective-permute-start.1 = (f32[1024,128]{0,1:T(8,128)S(1)}, f32[1024,128]{0,1:T(8,128)S(1)}, u32[]{:S(2)}, u32[]{:S(2)}) collective-permute-start(f32[1024,128]{0,1:T(8,128)S(1)} %add.111), channel_id=1, source_target_pairs={{0,2},{1,3},{2,0},{3,1},{4,6},{5,7},{6,4},{7,5},{8,10},{9,11},{10,... | collective-permute-start | bytes 1572872 | tf_op jit(solution)/shard_map/while/body/eval_jaxpr/ppermute | solution.py:48
  294.9 14.7 %collective-permute-start.2 = (f32[1024,128]{0,1:T(8,128)S(1)}, f32[1024,128]{0,1:T(8,128)S(1)}, u32[]{:S(2)}, u32[]{:S(2)}) collective-permute-start(f32[1024,128]{0,1:T(8,128)S(1)} %add.112), channel_id=1, source_target_pairs={{0,4},{1,5},{2,6},{3,7},{4,0},{5,1},{6,2},{7,3},{8,12},{9,13},{10,... | collective-permute-start | bytes 1572872 | tf_op jit(solution)/shard_map/while/body/eval_jaxpr/ppermute | solution.py:48
  362.4 14.7 %collective-permute-start.2 = (f32[1024,128]{0,1:T(8,128)S(1)}, f32[1024,128]{0,1:T(8,128)S(1)}, u32[]{:S(2)}, u32[]{:S(2)}) collective-permute-start(f32[1024,128]{0,1:T(8,128)S(1)} %add.112), channel_id=1, source_target_pairs={{0,4},{1,5},{2,6},{3,7},{4,0},{5,1},{6,2},{7,3},{8,12},{9,13},{10,... | collective-permute-start | bytes 1572872 | tf_op jit(solution)/shard_map/while/body/eval_jaxpr/ppermute | solution.py:48
  416.1 14.1 %collective-permute-start.1 = (f32[1024,128]{0,1:T(8,128)S(1)}, f32[1024,128]{0,1:T(8,128)S(1)}, u32[]{:S(2)}, u32[]{:S(2)}) collective-permute-start(f32[1024,128]{0,1:T(8,128)S(1)} %add.111), channel_id=1, source_target_pairs={{0,2},{1,3},{2,0},{3,1},{4,6},{5,7},{6,4},{7,5},{8,10},{9,11},{10,... | collective-permute-start | bytes 1572872 | tf_op jit(solution)/shard_map/while/body/eval_jaxpr/ppermute | solution.py:48
  430.2 14.7 %collective-permute-start.2 = (f32[1024,128]{0,1:T(8,128)S(1)}, f32[1024,128]{0,1:T(8,128)S(1)}, u32[]{:S(2)}, u32[]{:S(2)}) collective-permute-start(f32[1024,128]{0,1:T(8,128)S(1)} %add.112), channel_id=1, source_target_pairs={{0,4},{1,5},{2,6},{3,7},{4,0},{5,1},{6,2},{7,3},{8,12},{9,13},{10,... | collective-permute-start | bytes 1572872 | tf_op jit(solution)/shard_map/while/body/eval_jaxpr/ppermute | solution.py:48
  498.1 14.7 %collective-permute-start.2 = (f32[1024,128]{0,1:T(8,128)S(1)}, f32[1024,128]{0,1:T(8,128)S(1)}, u32[]{:S(2)}, u32[]{:S(2)}) collective-permute-start(f32[1024,128]{0,1:T(8,128)S(1)} %add.112), channel_id=1, source_target_pairs={{0,4},{1,5},{2,6},{3,7},{4,0},{5,1},{6,2},{7,3},{8,12},{9,13},{10,... | collective-permute-start | bytes 1572872 | tf_op jit(solution)/shard_map/while/body/eval_jaxpr/ppermute | solution.py:48
  565.9 14.7 %collective-permute-start.2 = (f32[1024,128]{0,1:T(8,128)S(1)}, f32[1024,128]{0,1:T(8,128)S(1)}, u32[]{:S(2)}, u32[]{:S(2)}) collective-permute-start(f32[1024,128]{0,1:T(8,128)S(1)} %add.112), channel_id=1, source_target_pairs={{0,4},{1,5},{2,6},{3,7},{4,0},{5,1},{6,2},{7,3},{8,12},{9,13},{10,... | collective-permute-start | bytes 1572872 | tf_op jit(solution)/shard_map/while/body/eval_jaxpr/ppermute | solution.py:48
  633.7 14.7 %collective-permute-start.2 = (f32[1024,128]{0,1:T(8,128)S(1)}, f32[1024,128]{0,1:T(8,128)S(1)}, u32[]{:S(2)}, u32[]{:S(2)}) collective-permute-start(f32[1024,128]{0,1:T(8,128)S(1)} %add.112), channel_id=1, source_target_pairs={{0,4},{1,5},{2,6},{3,7},{4,0},{5,1},{6,2},{7,3},{8,12},{9,13},{10,... | collective-permute-start | bytes 1572872 | tf_op jit(solution)/shard_map/while/body/eval_jaxpr/ppermute | solution.py:48
  687.5 14.1 %collective-permute-start.1 = (f32[1024,128]{0,1:T(8,128)S(1)}, f32[1024,128]{0,1:T(8,128)S(1)}, u32[]{:S(2)}, u32[]{:S(2)}) collective-permute-start(f32[1024,128]{0,1:T(8,128)S(1)} %add.111), channel_id=1, source_target_pairs={{0,2},{1,3},{2,0},{3,1},{4,6},{5,7},{6,4},{7,5},{8,10},{9,11},{10,... | collective-permute-start | bytes 1572872 | tf_op jit(solution)/shard_map/while/body/eval_jaxpr/ppermute | solution.py:48
  701.6 14.7 %collective-permute-start.2 = (f32[1024,128]{0,1:T(8,128)S(1)}, f32[1024,128]{0,1:T(8,128)S(1)}, u32[]{:S(2)}, u32[]{:S(2)}) collective-permute-start(f32[1024,128]{0,1:T(8,128)S(1)} %add.112), channel_id=1, source_target_pairs={{0,4},{1,5},{2,6},{3,7},{4,0},{5,1},{6,2},{7,3},{8,12},{9,13},{10,... | collective-permute-start | bytes 1572872 | tf_op jit(solution)/shard_map/while/body/eval_jaxpr/ppermute | solution.py:48
  755.3 14.1 %collective-permute-start.1 = (f32[1024,128]{0,1:T(8,128)S(1)}, f32[1024,128]{0,1:T(8,128)S(1)}, u32[]{:S(2)}, u32[]{:S(2)}) collective-permute-start(f32[1024,128]{0,1:T(8,128)S(1)} %add.111), channel_id=1, source_target_pairs={{0,2},{1,3},{2,0},{3,1},{4,6},{5,7},{6,4},{7,5},{8,10},{9,11},{10,... | collective-permute-start | bytes 1572872 | tf_op jit(solution)/shard_map/while/body/eval_jaxpr/ppermute | solution.py:48
  769.4 14.7 %collective-permute-start.2 = (f32[1024,128]{0,1:T(8,128)S(1)}, f32[1024,128]{0,1:T(8,128)S(1)}, u32[]{:S(2)}, u32[]{:S(2)}) collective-permute-start(f32[1024,128]{0,1:T(8,128)S(1)} %add.112), channel_id=1, source_target_pairs={{0,4},{1,5},{2,6},{3,7},{4,0},{5,1},{6,2},{7,3},{8,12},{9,13},{10,... | collective-permute-start | bytes 1572872 | tf_op jit(solution)/shard_map/while/body/eval_jaxpr/ppermute | solution.py:48
  837.3 14.7 %collective-permute-start.2 = (f32[1024,128]{0,1:T(8,128)S(1)}, f32[1024,128]{0,1:T(8,128)S(1)}, u32[]{:S(2)}, u32[]{:S(2)}) collective-permute-start(f32[1024,128]{0,1:T(8,128)S(1)} %add.112), channel_id=1, source_target_pairs={{0,4},{1,5},{2,6},{3,7},{4,0},{5,1},{6,2},{7,3},{8,12},{9,13},{10,... | collective-permute-start | bytes 1572872 | tf_op jit(solution)/shard_map/while/body/eval_jaxpr/ppermute | solution.py:48
  905.2 14.7 %collective-permute-start.2 = (f32[1024,128]{0,1:T(8,128)S(1)}, f32[1024,128]{0,1:T(8,128)S(1)}, u32[]{:S(2)}, u32[]{:S(2)}) collective-permute-start(f32[1024,128]{0,1:T(8,128)S(1)} %add.112), channel_id=1, source_target_pairs={{0,4},{1,5},{2,6},{3,7},{4,0},{5,1},{6,2},{7,3},{8,12},{9,13},{10,... | collective-permute-start | bytes 1572872 | tf_op jit(solution)/shard_map/while/body/eval_jaxpr/ppermute | solution.py:48
  973.0 14.7 %collective-permute-start.2 = (f32[1024,128]{0,1:T(8,128)S(1)}, f32[1024,128]{0,1:T(8,128)S(1)}, u32[]{:S(2)}, u32[]{:S(2)}) collective-permute-start(f32[1024,128]{0,1:T(8,128)S(1)} %add.112), channel_id=1, source_target_pairs={{0,4},{1,5},{2,6},{3,7},{4,0},{5,1},{6,2},{7,3},{8,12},{9,13},{10,... | collective-permute-start | bytes 1572872 | tf_op jit(solution)/shard_map/while/body/eval_jaxpr/ppermute | solution.py:48
  (85 other events, 813.7 us)
Sparse Core Ops, SparseCore 0:
  1028.1 50.1 reduce-scatter.1
